TPU v7x, 256 devices: a whole 4x4x8 slice. The times are simulated.
256 devices in a mesh: row: 8 (over z_hi, y), col: 32 (over x, z_lo, core).
Axes of the slice: x: 4, y: 4, z: 8 (z_hi: 2, z_lo: 4; z = z_hi * 4 + z_lo), core: 2. Of those that a mesh axis runs over, the one named last changes fastest.
Arguments:
- features: bfloat16 [65536, 256], P('col', 'row'), may hold values from -6 to 6
- block_values: bfloat16 [8, 32, 256, 128, 128], P('row', 'col'), may hold values from -0.046875 to 0.046875
- block_coords: int32 [8, 32, 2, 256], P('row', 'col'), may hold values from 0 to 63, as said below
- live_blocks: int32 [8, 32], P('row', 'col'), may hold values from 32 to 256, as said below
- weight: bfloat16 [256, 256], replicated, may hold values from -0.375 to 0.375
- bias: float32 [256], replicated, may hold values from -3 to 3
- cotangent: bfloat16 [65536, 256], P(('row', 'col')), may hold values from -6 to 6
Outputs:
- out: bfloat16 [65536, 256], P(('row', 'col'))
- grad_x: bfloat16 [65536, 256], P('col', 'row')
- grad_weight: float32 [256, 256], replicated
- grad_bias: float32 [256], replicated
Inputs may be any that keep to these rules, and one draw needn't show every extreme that they name: `block_coords`: within one tile the 256 slots name distinct pairs of a row block (0 to 63) and a column block (0 to 15). Only the first live_blocks[i, j] slots of tile (i, j) belong to the adjacency; some tile has all 256 slots live.
All inputs are finite; a program needn't handle non-finite values.
Results may differ from a plain program's by a relative error of at most 0.0075.
Values may be sent and summed in bfloat16 or wider, within the bound.
A program may use at most 128 MiB of HBM per device.

v0:
```python
import math
import jax
import jax.numpy as jnp
from jax import lax
from jax.sharding import PartitionSpec as P


def block_products(block_vals, source, dst_index, src_index, live_count, out_blocks, transposed):
    slot_total = block_vals.shape[0]
    block_size = block_vals.shape[1]
    feat_width = source.shape[2]
    group_size = math.gcd(slot_total, 64)
    pattern = "sab,saf->sbf" if transposed else "sab,sbf->saf"
    offsets = jnp.arange(group_size, dtype=jnp.int32)

    def one_group(turn, totals):
        first_slot = turn * group_size
        slab_vals = lax.dynamic_slice_in_dim(block_vals, first_slot, group_size, 0)
        take_from = lax.dynamic_slice_in_dim(src_index, first_slot, group_size, 0)
        put_to = lax.dynamic_slice_in_dim(dst_index, first_slot, group_size, 0)
        picked = jnp.take(source, take_from, axis=0)
        products = jnp.einsum(pattern, slab_vals, picked, preferred_element_type=jnp.float32)
        alive_mask = first_slot + offsets < live_count
        products = jnp.where(alive_mask[:, None, None], products, 0.0)
        return totals.at[put_to].add(products)

    start_totals = jnp.zeros((out_blocks, block_size, feat_width), jnp.float32)
    turns = slot_total // group_size
    return lax.fori_loop(0, turns, one_group, start_totals)


def on_device(features, block_values, block_coords, live_blocks, weight, bias, cotangent):
    block_vals = block_values[0, 0]
    row_ids = block_coords[0, 0, 0]
    col_ids = block_coords[0, 0, 1]
    live_count = live_blocks[0, 0]
    block_size = block_vals.shape[1]
    feat_width = weight.shape[0]
    col_count = lax.axis_size("col")
    feat_tile = lax.all_gather(features, "row", axis=1, tiled=True)
    col_blocks = feat_tile.shape[0] // block_size
    row_blocks = cotangent.shape[0] * col_count // block_size
    feat_blocks = feat_tile.reshape(col_blocks, block_size, feat_width)
    partial_value = block_products(
        block_vals, feat_blocks, row_ids, col_ids, live_count, row_blocks, False
    )
    partial_value = partial_value.reshape(row_blocks * block_size, feat_width)
    aggregate = lax.psum_scatter(partial_value, "col", scatter_dimension=0, tiled=True).astype(
        jnp.bfloat16
    )
    preact = jnp.dot(aggregate, weight, preferred_element_type=jnp.float32) + bias
    sigmoid_v = jax.nn.sigmoid(preact)
    out = (preact * sigmoid_v).astype(jnp.bfloat16)
    derivative = sigmoid_v * (1.0 + preact * (1.0 - sigmoid_v))
    grad_pre = (cotangent.astype(jnp.float32) * derivative).astype(jnp.bfloat16)
    weight_term = lax.dot_general(
        aggregate, grad_pre, (((0,), (0,)), ((), ())), preferred_element_type=jnp.float32
    )
    bias_term = jnp.sum(grad_pre.astype(jnp.float32), axis=0)
    weight_sum, bias_sum = lax.psum((weight_term, bias_term), ("row", "col"))
    norm_factor = (feat_tile.shape[0] * col_count) ** (-0.5)
    grad_weight = weight_sum * norm_factor
    grad_bias = bias_sum * norm_factor
    grad_agg = lax.dot_general(
        grad_pre, weight, (((1,), (1,)), ((), ())), preferred_element_type=jnp.float32
    ).astype(jnp.bfloat16)
    grad_tile = lax.all_gather(grad_agg, "col", axis=0, tiled=True)
    grad_blocks = grad_tile.reshape(row_blocks, block_size, feat_width)
    partial_x = block_products(
        block_vals, grad_blocks, col_ids, row_ids, live_count, col_blocks, True
    )
    partial_x = partial_x.reshape(col_blocks * block_size, feat_width)
    grad_x = lax.psum_scatter(partial_x, "row", scatter_dimension=1, tiled=True).astype(
        jnp.bfloat16
    )
    return (out, grad_x, grad_weight, grad_bias)


def solution(mesh):
    in_specs = (
        P("col", "row"),
        P("row", "col", None, None, None),
        P("row", "col", None, None),
        P("row", "col"),
        P(),
        P(),
        P(("row", "col"), None),
    )
    out_specs = (P(("row", "col"), None), P("col", "row"), P(), P())
    return jax.shard_map(
        on_device, mesh=mesh, in_specs=in_specs, out_specs=out_specs, check_vma=False
    )
```

profile of v0, /device:TPU:2, one launch (start us, length us, event | category | flops | bytes accessed | tf_op | source)
XLA Modules:
  0.0 785.1 jit_solution(2173765968436024874)
XLA Ops:
  8.0 0.8 fusion.27
  8.7 66.8 %all-gather.3.cloned.1.call-done = bf16[2048,256]{0,1:T(8,128)(2,1)} async-done(((bf16[2048,32]{0,1:T(8,128)(2,1)}), bf16[2048,256]{0,1:T(8,128)(2,1)}) %all-gather.3.cloned.1.call-update) | async-done | bytes 1048592 | tf_op jit(solution)/shard_map/all_gather | solution.py:40
  75.5 1.5 copy.12
  77.0 4.2 broadcast_in_dim.123
  81.3 122.0 %while.28 = (s32[]{:T(128)}, f32[64,128,256]{2,1,0:T(8,128)}, s32[256]{0:T(256)S(1)}, s32[]{:T(128)}, bf16[256,128,128]{2,1,0:T(8,128)(2,1)}, /*index=5*/s32[256...) while((s32[]{:T(128)}, f32[64,128,256]{2,1,0:T(8,128)}, ...), condition=%wide.region_2.3_spmd.clone, body=%wide.region_0.2_spmd.clone.sunk | while | flops 543164096 | bytes 48240816 | solution.py:29
  82.0 2.8 gather_fusion
  84.8 7.4 broadcast_select_fusion.4
  92.2 19.6 %scatter_fusion = f32[64,128,256]{2,1,0:T(8,128)} fusion(f32[64,128,256]{2,1,0:T(8,128)} %get-tuple-element.472, s32[64]{0:T(128)S(1)} %compare_select_fusion.8, f32[64,128,256]{2,1,0:T(8,128)} %broadcast_select_fusion.4), kind=kCustom, calls=%fused_computation.2.clone.clone.1 | custom fusion | flops 2097152 | bytes 25166080 | tf_op jit(solution)/shard_map/while/body/eval_jaxpr/scatter-add | solution.py:25
  112.6 2.8 gather_fusion
  115.3 7.4 broadcast_select_fusion.4
  122.8 19.4 %scatter_fusion = f32[64,128,256]{2,1,0:T(8,128)} fusion(f32[64,128,256]{2,1,0:T(8,128)} %get-tuple-element.472, s32[64]{0:T(128)S(1)} %compare_select_fusion.8, f32[64,128,256]{2,1,0:T(8,128)} %broadcast_select_fusion.4), kind=kCustom, calls=%fused_computation.2.clone.clone.1 | custom fusion | flops 2097152 | bytes 25166080 | tf_op jit(solution)/shard_map/while/body/eval_jaxpr/scatter-add | solution.py:25
  142.2 0.7 compare_and_fusion.4
  142.9 2.8 gather_fusion
  145.7 7.4 broadcast_select_fusion.4
  153.1 19.6 %scatter_fusion = f32[64,128,256]{2,1,0:T(8,128)} fusion(f32[64,128,256]{2,1,0:T(8,128)} %get-tuple-element.472, s32[64]{0:T(128)S(1)} %compare_select_fusion.8, f32[64,128,256]{2,1,0:T(8,128)} %broadcast_select_fusion.4), kind=kCustom, calls=%fused_computation.2.clone.clone.1 | custom fusion | flops 2097152 | bytes 25166080 | tf_op jit(solution)/shard_map/while/body/eval_jaxpr/scatter-add | solution.py:25
  172.7 0.7 compare_and_fusion.4
  173.5 2.8 gather_fusion
  176.2 7.4 broadcast_select_fusion.4
  183.6 19.6 %scatter_fusion = f32[64,128,256]{2,1,0:T(8,128)} fusion(f32[64,128,256]{2,1,0:T(8,128)} %get-tuple-element.472, s32[64]{0:T(128)S(1)} %compare_select_fusion.8, f32[64,128,256]{2,1,0:T(8,128)} %broadcast_select_fusion.4), kind=kCustom, calls=%fused_computation.2.clone.clone.1 | custom fusion | flops 2097152 | bytes 25166080 | tf_op jit(solution)/shard_map/while/body/eval_jaxpr/scatter-add | solution.py:25
  203.3 138.4 %reduce-scatter.3.cloned.1.call-done = f32[256,256]{1,0:T(8,128)} async-done(((f32[8192,256]{1,0:T(8,128)}), f32[256,256]{1,0:T(8,128)}) %reduce-scatter.3.cloned.1.call-update) | async-done | bytes 262160 | tf_op jit(solution)/shard_map/reduce_scatter | solution.py:48
  341.7 1.9 convert_reduce_fusion
  343.6 0.9 convolution_convert_fusion
  344.6 12.0 %copy.11 = bf16[1,1,256,128,128]{3,4,2,1,0:T(8,128)(2,1)} copy(bf16[1,1,256,128,128]{4,3,2,1,0:T(8,128)(2,1)} %bitcast.18) | data formatting | bytes 16777216 | tf_op args[1]
  356.6 0.9 fusion.24
  357.6 65.8 %all-gather.5.cloned.1.call-done = bf16[8192,256]{1,0:T(8,128)(2,1)} async-done(((bf16[256,256]{1,0:T(8,128)(2,1)}), bf16[8192,256]{1,0:T(8,128)(2,1)}) %all-gather.5.cloned.1.call-update) | async-done | bytes 4194320 | tf_op jit(solution)/shard_map/all_gather | solution.py:67
  423.6 102.6 %while.29 = (s32[]{:T(128)}, f32[16,128,256]{2,1,0:T(8,128)S(1)}, s32[256]{0:T(256)S(1)}, s32[]{:T(128)}, bf16[256,128,128]{1,2,0:T(8,128)(2,1)}, /*index=5*/s32...) while((s32[]{:T(128)}, f32[16,128,256]{2,1,0:T(8,128)S(1)}, ...), condition=%wide.region_6.7_spmd.clone, body=%wide.region_4.6_spmd.clone.sunk | while | flops 543164096 | bytes 48240816 | solution.py:29
  423.7 0.7 compare_and_fusion.5
  424.4 5.0 gather_fusion.1
  429.4 7.4 broadcast_select_fusion.5
  436.8 12.4 %scatter_fusion.1 = f32[16,128,256]{2,1,0:T(8,128)S(1)} fusion(f32[16,128,256]{2,1,0:T(8,128)S(1)} %get-tuple-element.505, s32[64]{0:T(128)S(1)} %compare_select_fusion.9, f32[64,128,256]{2,1,0:T(8,128)} %broadcast_select_fusion.5), kind=kCustom, calls=%fused_computation.3.clone.clone.1 | custom fusion | flops 2097152 | bytes 25166080 | tf_op jit(solution)/shard_map/while/body/eval_jaxpr/scatter-add | solution.py:25
  449.3 0.7 compare_and_fusion.5
  450.0 5.0 gather_fusion.1
  455.0 7.4 broadcast_select_fusion.5
  462.5 12.5 %scatter_fusion.1 = f32[16,128,256]{2,1,0:T(8,128)S(1)} fusion(f32[16,128,256]{2,1,0:T(8,128)S(1)} %get-tuple-element.505, s32[64]{0:T(128)S(1)} %compare_select_fusion.9, f32[64,128,256]{2,1,0:T(8,128)} %broadcast_select_fusion.5), kind=kCustom, calls=%fused_computation.3.clone.clone.1 | custom fusion | flops 2097152 | bytes 25166080 | tf_op jit(solution)/shard_map/while/body/eval_jaxpr/scatter-add | solution.py:25
  475.0 0.7 compare_and_fusion.5
  475.7 5.0 gather_fusion.1
  480.7 7.4 broadcast_select_fusion.5
  488.2 12.4 %scatter_fusion.1 = f32[16,128,256]{2,1,0:T(8,128)S(1)} fusion(f32[16,128,256]{2,1,0:T(8,128)S(1)} %get-tuple-element.505, s32[64]{0:T(128)S(1)} %compare_select_fusion.9, f32[64,128,256]{2,1,0:T(8,128)} %broadcast_select_fusion.5), kind=kCustom, calls=%fused_computation.3.clone.clone.1 | custom fusion | flops 2097152 | bytes 25166080 | tf_op jit(solution)/shard_map/while/body/eval_jaxpr/scatter-add | solution.py:25
  500.6 0.7 compare_and_fusion.5
  501.3 5.0 gather_fusion.1
  506.3 7.4 broadcast_select_fusion.5
  513.8 12.4 %scatter_fusion.1 = f32[16,128,256]{2,1,0:T(8,128)S(1)} fusion(f32[16,128,256]{2,1,0:T(8,128)S(1)} %get-tuple-element.505, s32[64]{0:T(128)S(1)} %compare_select_fusion.9, f32[64,128,256]{2,1,0:T(8,128)} %broadcast_select_fusion.5), kind=kCustom, calls=%fused_computation.3.clone.clone.1 | custom fusion | flops 2097152 | bytes 25166080 | tf_op jit(solution)/shard_map/while/body/eval_jaxpr/scatter-add | solution.py:25
  526.2 1.9 copy.16
  528.1 76.1 %psum.15 = f32[256]{0:T(256)S(1)} all-reduce(f32[256]{0:T(256)S(1)} %get-tuple-element.355), channel_id=1, replica_groups=mesh['row'=8,'col'=32] {'row','col'}, use_global_device_ids=true, to_apply=%region_10.11 | all-reduce | flops 256 | bytes 2048 | tf_op jit(solution)/shard_map/psum | solution.py:60
  604.8 74.2 %all-reduce.2.cloned.1.call-done = f32[256,256]{1,0:T(8,128)} async-done(((f32[256,256]{1,0:T(8,128)}), f32[256,256]{1,0:T(8,128)}) %all-reduce.2.cloned.1.call-update) | async-done | bytes 262160 | tf_op jit(solution)/shard_map/psum | solution.py:60
  679.0 1.7 broadcast_multiply_fusion
  680.7 96.3 %reduce-scatter.5.cloned.1.call-done = f32[2048,32]{0,1:T(8,128)} async-done(((f32[2048,256]{0,1:T(8,128)}), f32[2048,32]{0,1:T(8,128)}) %reduce-scatter.5.cloned.1.call-update) | async-done | bytes 262160 | tf_op jit(solution)/shard_map/reduce_scatter | solution.py:73
  776.9 1.6 convert_element_type.26
  (38 shorter events, 3.8 us)
Async XLA Ops:
  7.2 334.6 %copy-start = (bf16[256,256]{1,0:T(8,128)(2,1)S(1)}, bf16[256,256]{1,0:T(8,128)(2,1)}, u32[]{:S(2)}) copy-start(bf16[256,256]{1,0:T(8,128)(2,1)} %param.15) | copy-start | bytes 393220
  7.2 68.4 %all-gather.3.cloned.1.call-start = ((), (), s32[]{:S(2)}) async-start(), calls=%async_computation.2 | async-start | bytes 1179648 | tf_op jit(solution)/shard_map/all_gather | solution.py:40
  7.9 333.8 %reduce-scatter.3.cloned.1.call-start = ((), (), s32[]{:S(2)}) async-start(), calls=%async_computation.3 | async-start | bytes 8650752 | tf_op jit(solution)/shard_map/reduce_scatter | solution.py:48
  203.3 138.5 %copy-start.2 = (bf16[256,256]{1,0:T(8,128)(2,1)S(1)}, bf16[256,256]{1,0:T(8,128)(2,1)}, u32[]{:S(2)}) copy-start(bf16[256,256]{1,0:T(8,128)(2,1)} %param.17) | copy-start | bytes 393220
  203.3 138.5 %copy-start.3 = (f32[256]{0:T(256)S(1)}, f32[256]{0:T(256)}, u32[]{:S(2)}) copy-start(f32[256]{0:T(256)} %param.16) | copy-start | bytes 3076
  203.3 220.1 %all-gather.5.cloned.1.call-start = ((), (), s32[]{:S(2)}) async-start(), calls=%async_computation.4 | async-start | bytes 4325376 | tf_op jit(solution)/shard_map/all_gather | solution.py:67
  344.5 12.1 %copy-start.1 = (f32[256,256]{1,0:T(8,128)S(1)}, f32[256,256]{1,0:T(8,128)}, u32[]{:S(2)}) copy-start(f32[256,256]{1,0:T(8,128)} %reduce-scatter.3.cloned.1.call-done) | copy-start | bytes 786436
  344.5 334.4 %all-reduce.2.cloned.1.call-start = ((), (), s32[]{:S(2)}) async-start(), calls=%async_computation.6 | async-start | bytes 524288 | tf_op jit(solution)/shard_map/psum | solution.py:60
  357.5 419.4 %reduce-scatter.5.cloned.1.call-start = ((), (), s32[]{:S(2)}) async-start(), calls=%async_computation.5 | async-start | bytes 2359296 | tf_op jit(solution)/shard_map/reduce_scatter | solution.py:73
Sparse Core Ops, SparseCore 0:
  10.6 64.8 all-gather.2
  203.4 138.2 reduce-scatter.2
  344.7 78.7 all-gather.4
  429.3 249.6 all-reduce.1
  682.9 93.9 reduce-scatter.4
where the time goes:
time: 787 us; the launch traced here: 785 us
  waiting for transfers between devices  442 us (56%)
  other arithmetic  138 us (18%)
  blocking collectives  76.1 us (10%)
  matrix products  62.7 us (8%)
  local copies, waits for them, and re-layouts  51.5 us (7%)
  between operations  13.8 us (2%)
    reduce_scatter x1, waiting for transfers between devices, on_device(): lax.psum_scatter(partial_value, 'col', scatter_dimension=0, tiled=True)  138 us
    scatter-add x8, other arithmetic, one_group(): return totals.at[put_to].add(products)  128 us
    reduce_scatter x1, waiting for transfers between devices, on_device(): lax.psum_scatter(partial_x, 'row', scatter_dimension=1, tiled=True)  96.3 us
    psum x1, blocking collectives, on_device(): weight_sum, bias_sum = lax.psum((weight_term, bias_term), ('row', 'col'))  76.1 us
    psum x1, waiting for transfers between devices, on_device(): weight_sum, bias_sum = lax.psum((weight_term, bias_term), ('row', 'col'))  74.2 us
    all_gather x1, waiting for transfers between devices, on_device(): feat_tile = lax.all_gather(features, 'row', axis=1, tiled=True)  66.8 us
    all_gather x1, waiting for transfers between devices, on_device(): grad_tile = lax.all_gather(grad_agg, 'col', axis=0, tiled=True)  65.8 us
    dot_general x8, matrix products, one_group(): jnp.einsum(pattern, slab_vals, picked, preferred_element_type=jnp.float32)  59 us
  transfers between devices with their start and end apart: 5, of which 5 were waited for; matrix products, arithmetic and copies ran while one was open for 15% of the time, Pallas kernels for 0%

commit v1 on v0

--- a/solution.py
+++ b/solution.py
@@ -64,7 +64,9 @@
     grad_agg = lax.dot_general(
         grad_pre, weight, (((1,), (1,)), ((), ())), preferred_element_type=jnp.float32
     ).astype(jnp.bfloat16)
-    grad_tile = lax.all_gather(grad_agg, "col", axis=0, tiled=True)
+    grad_tile = jnp.concatenate(
+        lax.all_to_all(jnp.stack([grad_agg] * lax.axis_size("col")), "col", 0, 0), axis=0
+    )
     grad_blocks = grad_tile.reshape(row_blocks, block_size, feat_width)
     partial_x = block_products(
         block_vals, grad_blocks, col_ids, row_ids, live_count, col_blocks, True

time: 787 us -> 752 us (0.956)
  waiting for transfers between devices: 442 us -> 382 us
  starting transfers between devices: 0.2 us -> 25 us
    all_to_all x0 -> x1, waiting for transfers between devices: none -> 81 us  [on_device(): lax.all_to_all(jnp.stack([grad_agg] * lax.axis_size('col')), 'col', 0, 0)]
    psum x1, waiting for transfers between devices: 74.2 us -> 0.01 us  [on_device(): weight_sum, bias_sum = lax.psum((weight_term, bias_term), ('row', 'col'))]
    all_gather x1 -> x0, waiting for transfers between devices: 65.8 us -> none  [on_device(): grad_tile = lax.all_gather(grad_agg, 'col', axis=0, tiled=True)]
    all_to_all x0 -> x1, starting transfers between devices: none -> 24.9 us  [on_device(): lax.all_to_all(jnp.stack([grad_agg] * lax.axis_size('col')), 'col', 0, 0)]
  transfers between devices with their start and end apart: 5 -> 5, of which waited for: 5 -> 4; matrix products, arithmetic and copies ran while one was open for 15% -> 16% of each run, Pallas kernels for 0% -> 0%
where the time goes in v1:
time: 752 us; the launch traced here: 750 us
  waiting for transfers between devices  382 us (51%)
  other arithmetic  138 us (18%)
  blocking collectives  75 us (10%)
  matrix products  62 us (8%)
  local copies, waits for them, and re-layouts  53.8 us (7%)
  starting transfers between devices  25 us (3%)
  between operations  13.8 us (2%)
    reduce_scatter x1, waiting for transfers between devices, on_device(): lax.psum_scatter(partial_value, 'col', scatter_dimension=0, tiled=True)  139 us
    scatter-add x8, other arithmetic, one_group(): return totals.at[put_to].add(products)  128 us
    reduce_scatter x1, waiting for transfers between devices, on_device(): lax.psum_scatter(partial_x, 'row', scatter_dimension=1, tiled=True)  95 us
    all_to_all x1, waiting for transfers between devices, on_device(): lax.all_to_all(jnp.stack([grad_agg] * lax.axis_size('col')), 'col', 0, 0)  81 us
    psum x1, blocking collectives, on_device(): weight_sum, bias_sum = lax.psum((weight_term, bias_term), ('row', 'col'))  75 us
    all_gather x1, waiting for transfers between devices, on_device(): feat_tile = lax.all_gather(features, 'row', axis=1, tiled=True)  66.8 us
    dot_general x8, matrix products, one_group(): jnp.einsum(pattern, slab_vals, picked, preferred_element_type=jnp.float32)  59 us
    gather x8, local copies, waits for them, and re-layouts, one_group(): picked = jnp.take(source, take_from, axis=0)  30.9 us
  transfers between devices with their start and end apart: 5, of which 4 were waited for; matrix products, arithmetic and copies ran while one was open for 16% of the time, Pallas kernels for 0%

profile of v1, /device:TPU:2, one launch (start us, length us, event | category | flops | bytes accessed | tf_op | source)
XLA Modules:
  0.0 750.5 jit_solution(5487249238387106441)
XLA Ops:
  8.0 0.8 fusion.27
  8.7 66.8 %all-gather.2.cloned.1.call-done = bf16[2048,256]{0,1:T(8,128)(2,1)} async-done(((bf16[2048,32]{0,1:T(8,128)(2,1)}), bf16[2048,256]{0,1:T(8,128)(2,1)}) %all-gather.2.cloned.1.call-update) | async-done | bytes 1048592 | tf_op jit(solution)/shard_map/all_gather | solution.py:40
  75.5 1.5 copy.12
  77.0 4.2 broadcast_in_dim.123
  81.3 122.0 %while.28 = (s32[]{:T(128)}, f32[64,128,256]{2,1,0:T(8,128)}, s32[256]{0:T(256)S(1)}, s32[]{:T(128)}, bf16[256,128,128]{2,1,0:T(8,128)(2,1)}, /*index=5*/s32[256...) while((s32[]{:T(128)}, f32[64,128,256]{2,1,0:T(8,128)}, ...), condition=%wide.region_2.3_spmd.clone, body=%wide.region_0.2_spmd.clone.sunk | while | flops 543164096 | bytes 48240816 | solution.py:29
  81.3 0.7 compare_and_fusion.4
  82.0 2.8 gather_fusion
  84.7 7.4 broadcast_select_fusion.4
  92.2 19.6 %scatter_fusion = f32[64,128,256]{2,1,0:T(8,128)} fusion(f32[64,128,256]{2,1,0:T(8,128)} %get-tuple-element.472, s32[64]{0:T(128)S(1)} %compare_select_fusion.8, f32[64,128,256]{2,1,0:T(8,128)} %broadcast_select_fusion.4), kind=kCustom, calls=%fused_computation.2.clone.clone.1 | custom fusion | flops 2097152 | bytes 25166080 | tf_op jit(solution)/shard_map/while/body/eval_jaxpr/scatter-add | solution.py:25
  112.6 2.8 gather_fusion
  115.3 7.4 broadcast_select_fusion.4
  122.8 19.4 %scatter_fusion = f32[64,128,256]{2,1,0:T(8,128)} fusion(f32[64,128,256]{2,1,0:T(8,128)} %get-tuple-element.472, s32[64]{0:T(128)S(1)} %compare_select_fusion.8, f32[64,128,256]{2,1,0:T(8,128)} %broadcast_select_fusion.4), kind=kCustom, calls=%fused_computation.2.clone.clone.1 | custom fusion | flops 2097152 | bytes 25166080 | tf_op jit(solution)/shard_map/while/body/eval_jaxpr/scatter-add | solution.py:25
  142.2 0.7 compare_and_fusion.4
  142.9 2.8 gather_fusion
  145.7 7.4 broadcast_select_fusion.4
  153.1 19.6 %scatter_fusion = f32[64,128,256]{2,1,0:T(8,128)} fusion(f32[64,128,256]{2,1,0:T(8,128)} %get-tuple-element.472, s32[64]{0:T(128)S(1)} %compare_select_fusion.8, f32[64,128,256]{2,1,0:T(8,128)} %broadcast_select_fusion.4), kind=kCustom, calls=%fused_computation.2.clone.clone.1 | custom fusion | flops 2097152 | bytes 25166080 | tf_op jit(solution)/shard_map/while/body/eval_jaxpr/scatter-add | solution.py:25
  173.5 2.8 gather_fusion
  176.2 7.4 broadcast_select_fusion.4
  183.6 19.6 %scatter_fusion = f32[64,128,256]{2,1,0:T(8,128)} fusion(f32[64,128,256]{2,1,0:T(8,128)} %get-tuple-element.472, s32[64]{0:T(128)S(1)} %compare_select_fusion.8, f32[64,128,256]{2,1,0:T(8,128)} %broadcast_select_fusion.4), kind=kCustom, calls=%fused_computation.2.clone.clone.1 | custom fusion | flops 2097152 | bytes 25166080 | tf_op jit(solution)/shard_map/while/body/eval_jaxpr/scatter-add | solution.py:25
  203.3 138.8 %reduce-scatter.3.cloned.1.call-done = f32[256,256]{1,0:T(8,128)} async-done(((f32[8192,256]{1,0:T(8,128)}), f32[256,256]{1,0:T(8,128)}) %reduce-scatter.3.cloned.1.call-update) | async-done | bytes 262160 | tf_op jit(solution)/shard_map/reduce_scatter | solution.py:48
  342.1 1.9 convert_reduce_fusion
  344.2 2.4 stack.2
  346.6 24.9 %all-to-all-start = ((bf16[32,256,256]{2,1,0:T(8,128)(2,1)}), bf16[32,256,256]{2,1,0:T(8,128)(2,1)}, u32[]{:S(2)}, u32[]{:S(2)}) async-start(bf16[32,256,256]{2,1,0:T(8,128)(2,1)} %stack.2), calls=%async_computation.1 | async-start | bytes 8388608 | tf_op jit(solution)/shard_map/all_to_all | solution.py:68
  371.5 12.0 %copy.11 = bf16[1,1,256,128,128]{3,4,2,1,0:T(8,128)(2,1)} copy(bf16[1,1,256,128,128]{4,3,2,1,0:T(8,128)(2,1)} %bitcast.17) | data formatting | bytes 16777216 | tf_op args[1]
  383.5 0.9 fusion.24
  384.5 81.0 %all-to-all-done = bf16[32,256,256]{2,1,0:T(8,128)(2,1)} async-done(((bf16[32,256,256]{2,1,0:T(8,128)(2,1)}), bf16[32,256,256]{2,1,0:T(8,128)(2,1)}, u32[]{:S(2)}, u32[]{:S(2)}) %all-to-all-start) | async-done | bytes 4194336 | tf_op jit(solution)/shard_map/all_to_all | solution.py:68
  465.7 102.5 %while.29 = (s32[]{:T(128)}, f32[16,128,256]{2,1,0:T(8,128)S(1)}, s32[256]{0:T(256)S(1)}, s32[]{:T(128)}, bf16[256,128,128]{1,2,0:T(8,128)(2,1)}, /*index=5*/s32...) while((s32[]{:T(128)}, f32[16,128,256]{2,1,0:T(8,128)S(1)}, ...), condition=%wide.region_6.7_spmd.clone, body=%wide.region_4.6_spmd.clone.sunk | while | flops 543164096 | bytes 48240816 | solution.py:29
  465.8 0.7 compare_and_fusion.5
  466.5 5.0 gather_fusion.1
  471.5 7.4 broadcast_select_fusion.5
  478.9 12.4 %scatter_fusion.1 = f32[16,128,256]{2,1,0:T(8,128)S(1)} fusion(f32[16,128,256]{2,1,0:T(8,128)S(1)} %get-tuple-element.505, s32[64]{0:T(128)S(1)} %compare_select_fusion.9, f32[64,128,256]{2,1,0:T(8,128)} %broadcast_select_fusion.5), kind=kCustom, calls=%fused_computation.3.clone.clone.1 | custom fusion | flops 2097152 | bytes 25166080 | tf_op jit(solution)/shard_map/while/body/eval_jaxpr/scatter-add | solution.py:25
  491.4 0.7 compare_and_fusion.5
  492.1 5.0 gather_fusion.1
  497.1 7.4 broadcast_select_fusion.5
  504.6 12.4 %scatter_fusion.1 = f32[16,128,256]{2,1,0:T(8,128)S(1)} fusion(f32[16,128,256]{2,1,0:T(8,128)S(1)} %get-tuple-element.505, s32[64]{0:T(128)S(1)} %compare_select_fusion.9, f32[64,128,256]{2,1,0:T(8,128)} %broadcast_select_fusion.5), kind=kCustom, calls=%fused_computation.3.clone.clone.1 | custom fusion | flops 2097152 | bytes 25166080 | tf_op jit(solution)/shard_map/while/body/eval_jaxpr/scatter-add | solution.py:25
  517.0 0.7 compare_and_fusion.5
  517.8 5.0 gather_fusion.1
  522.7 7.4 broadcast_select_fusion.5
  530.2 12.4 %scatter_fusion.1 = f32[16,128,256]{2,1,0:T(8,128)S(1)} fusion(f32[16,128,256]{2,1,0:T(8,128)S(1)} %get-tuple-element.505, s32[64]{0:T(128)S(1)} %compare_select_fusion.9, f32[64,128,256]{2,1,0:T(8,128)} %broadcast_select_fusion.5), kind=kCustom, calls=%fused_computation.3.clone.clone.1 | custom fusion | flops 2097152 | bytes 25166080 | tf_op jit(solution)/shard_map/while/body/eval_jaxpr/scatter-add | solution.py:25
  542.7 0.7 compare_and_fusion.5
  543.4 5.0 gather_fusion.1
  548.4 7.4 broadcast_select_fusion.5
  555.8 12.4 %scatter_fusion.1 = f32[16,128,256]{2,1,0:T(8,128)S(1)} fusion(f32[16,128,256]{2,1,0:T(8,128)S(1)} %get-tuple-element.505, s32[64]{0:T(128)S(1)} %compare_select_fusion.9, f32[64,128,256]{2,1,0:T(8,128)} %broadcast_select_fusion.5), kind=kCustom, calls=%fused_computation.3.clone.clone.1 | custom fusion | flops 2097152 | bytes 25166080 | tf_op jit(solution)/shard_map/while/body/eval_jaxpr/scatter-add | solution.py:25
  568.3 1.9 copy.16
  570.1 75.0 %psum.15 = f32[256]{0:T(256)S(1)} all-reduce(f32[256]{0:T(256)S(1)} %get-tuple-element.355), channel_id=1, replica_groups=mesh['row'=8,'col'=32] {'row','col'}, use_global_device_ids=true, to_apply=%region_10.11 | all-reduce | flops 256 | bytes 2048 | tf_op jit(solution)/shard_map/psum | solution.py:60
  645.7 1.7 broadcast_multiply_fusion
  647.3 95.0 %reduce-scatter.5.cloned.1.call-done = f32[2048,32]{0,1:T(8,128)} async-done(((f32[2048,256]{0,1:T(8,128)}), f32[2048,32]{0,1:T(8,128)}) %reduce-scatter.5.cloned.1.call-update) | async-done | bytes 262160 | tf_op jit(solution)/shard_map/reduce_scatter | solution.py:75
  742.3 1.6 convert_element_type.26
  (40 shorter events, 4.0 us)
Async XLA Ops:
  7.2 334.9 %copy-start = (bf16[256,256]{1,0:T(8,128)(2,1)S(1)}, bf16[256,256]{1,0:T(8,128)(2,1)}, u32[]{:S(2)}) copy-start(bf16[256,256]{1,0:T(8,128)(2,1)} %param.15) | copy-start | bytes 393220
  7.2 68.4 %all-gather.2.cloned.1.call-start = ((), (), s32[]{:S(2)}) async-start(), calls=%async_computation.3 | async-start | bytes 1179648 | tf_op jit(solution)/shard_map/all_gather | solution.py:40
  7.9 334.1 %reduce-scatter.3.cloned.1.call-start = ((), (), s32[]{:S(2)}) async-start(), calls=%async_computation.4 | async-start | bytes 8650752 | tf_op jit(solution)/shard_map/reduce_scatter | solution.py:48
  203.3 138.8 %copy-start.3 = (bf16[256,256]{1,0:T(8,128)(2,1)S(1)}, bf16[256,256]{1,0:T(8,128)(2,1)}, u32[]{:S(2)}) copy-start(bf16[256,256]{1,0:T(8,128)(2,1)} %param.17) | copy-start | bytes 393220
  203.3 138.8 %copy-start.4 = (f32[256]{0:T(256)S(1)}, f32[256]{0:T(256)}, u32[]{:S(2)}) copy-start(f32[256]{0:T(256)} %param.16) | copy-start | bytes 3076
  346.6 118.9 %all-to-all-start = ((bf16[32,256,256]{2,1,0:T(8,128)(2,1)}), bf16[32,256,256]{2,1,0:T(8,128)(2,1)}, u32[]{:S(2)}, u32[]{:S(2)}) async-start(bf16[32,256,256]{2,1,0:T(8,128)(2,1)} %stack.2), calls=%async_computation.1 | async-start | bytes 8388608 | tf_op jit(solution)/shard_map/all_to_all | solution.py:68
  371.5 12.1 %copy-start.2 = (f32[256,256]{1,0:T(8,128)S(1)}, f32[256,256]{1,0:T(8,128)}, u32[]{:S(2)}) copy-start(f32[256,256]{1,0:T(8,128)} %reduce-scatter.3.cloned.1.call-done) | copy-start | bytes 786436
  371.5 274.2 %all-reduce.2.cloned.1.call-start = ((), (), s32[]{:S(2)}) async-start(), calls=%async_computation.6 | async-start | bytes 524288 | tf_op jit(solution)/shard_map/psum | solution.py:60
  384.5 357.8 %reduce-scatter.5.cloned.1.call-start = ((), (), s32[]{:S(2)}) async-start(), calls=%async_computation.5 | async-start | bytes 2359296 | tf_op jit(solution)/shard_map/reduce_scatter | solution.py:75
  568.2 175.7 %copy-start.1 = (bf16[256,256]{1,0:T(8,128)(2,1)S(1)}, bf16[256,256]{1,0:T(8,128)(2,1)}, u32[]{:S(2)}) copy-start(bf16[256,256]{1,0:T(8,128)(2,1)} %param.15) | copy-start | bytes 393220
Sparse Core Ops, SparseCore 0:
  10.6 64.8 all-gather.1
  203.4 138.6 reduce-scatter.2
  384.6 259.6 all-reduce.1
  648.2 94.0 reduce-scatter.4
